TPU v7x, 128 devices: a whole 4x4x4 slice. The times are simulated.
128 devices in a mesh: space: 16 (over y_hi, x, core), code: 4 (over z), clip: 2 (over y_lo).
Axes of the slice: x: 4, y: 4 (y_hi: 2, y_lo: 2; y = y_hi * 2 + y_lo), z: 4, core: 2. Of those that a mesh axis runs over, the one named last changes fastest.
Arguments:
- soft_weights: bfloat16 [2, 1024, 32, 8192], P('clip', 'space', None, 'code'), may hold values from 0.00029945374 to 0.029907227
- codebook: bfloat16 [8192, 256], P('code'), may hold values from -6 to 6
- kernel_one: bfloat16 [3, 3, 256, 512], replicated, may hold values from -0.125 to 0.125
- kernel_two: bfloat16 [3, 3, 512, 512], replicated, may hold values from -0.09375 to 0.09375
- cotangent: bfloat16 [2, 1024, 32, 512], P('clip', ('space', 'code')), may hold values from -16 to 16
Outputs:
- decoded: bfloat16 [2, 1024, 32, 512], P('clip', ('space', 'code'))
- grad_one: float32 [3, 3, 256, 512], P(None, None, None, ('space', 'code', 'clip'))
- grad_two: float32 [3, 3, 512, 512], P(None, None, None, ('space', 'code', 'clip'))
- grad_codebook: float32 [8192, 256], P('code')
All inputs are finite; a program needn't handle non-finite values.
Results may differ from a plain program's by a relative error of at most 0.02.
Values may be sent and summed in bfloat16 or wider, within the bound.
A program may use at most 192 MiB of HBM per device.

v0:
```python
import jax
import jax.numpy as jnp
from jax import lax
from jax.sharding import PartitionSpec as P


def with_halo(block, sides, width):
    for axis, dim in sides:
        count = lax.axis_size(axis)
        forward = [(i, i + 1) for i in range(count - 1)]
        backward = [(target, source) for source, target in forward]
        low = lax.ppermute(
            lax.slice_in_dim(block, block.shape[dim] - width, None, axis=dim), axis, forward
        )
        high = lax.ppermute(lax.slice_in_dim(block, 0, width, axis=dim), axis, backward)
        block = jnp.concatenate([low, block, high], axis=dim)
    return block


def extend(field):
    grown = with_halo(field, ((("space", "code"), 0),), 1)
    return jnp.pad(grown, ((0, 0), (1, 1), (0, 0)))


def taps_forward(padded, kernel):
    height = padded.shape[0] - 2
    breadth = padded.shape[1] - 2
    accum = jnp.zeros((height * breadth, kernel.shape[3]), jnp.float32)
    for first in range(3):
        for second in range(3):
            window = padded[first : first + height, second : second + breadth].reshape(
                height * breadth, -1
            )
            accum = accum + jnp.dot(
                window, kernel[first, second], preferred_element_type=jnp.float32
            )
    return accum.reshape(height, breadth, -1)


def taps_back(padded, kernel):
    height = padded.shape[0] - 2
    breadth = padded.shape[1] - 2
    accum = jnp.zeros((height * breadth, kernel.shape[2]), jnp.float32)
    for first in range(3):
        for second in range(3):
            window = padded[
                2 - first : 2 - first + height, 2 - second : 2 - second + breadth
            ].reshape(height * breadth, -1)
            accum = accum + jnp.dot(
                window, kernel[first, second].T, preferred_element_type=jnp.float32
            )
    return accum.reshape(height, breadth, -1)


def kernel_grad(padded, upstream):
    height = upstream.shape[0]
    breadth = upstream.shape[1]
    flat_up = upstream.reshape(height * breadth, -1)
    result = []
    for first in range(3):
        line = []
        for second in range(3):
            window = padded[first : first + height, second : second + breadth].reshape(
                height * breadth, -1
            )
            line.append(
                lax.dot_general(
                    window, flat_up, (((0,), (0,)), ((), ())), preferred_element_type=jnp.float32
                )
            )
        result.append(jnp.stack(line))
    return jnp.stack(result)


def on_device(soft_weights, codebook, kernel_one, kernel_two, cotangent):
    weights = soft_weights[0]
    upstream = cotangent[0]
    own_rows = upstream.shape[0]
    breadth = weights.shape[1]
    code_slice = weights.shape[2]
    partial_value = jnp.dot(
        weights.reshape(-1, code_slice), codebook, preferred_element_type=jnp.float32
    )
    partial_value = partial_value.reshape(weights.shape[0], breadth, -1)
    summed = lax.psum(partial_value, "code")
    owned = lax.dynamic_slice_in_dim(summed, lax.axis_index("code") * own_rows, own_rows, 0)
    embedded = owned.astype(jnp.bfloat16)
    embed_pad = extend(embedded)
    pre_one = taps_forward(embed_pad, kernel_one)
    hidden = jax.nn.silu(pre_one).astype(jnp.bfloat16)
    hidden_pad = extend(hidden)
    decoded = taps_forward(hidden_pad, kernel_two).astype(jnp.bfloat16)
    grad_hidden = taps_back(extend(upstream), kernel_two)
    sigma = jax.nn.sigmoid(pre_one)
    grad_pre = (grad_hidden * sigma * (1.0 + pre_one * (1.0 - sigma))).astype(jnp.bfloat16)
    grad_embedded = taps_back(extend(grad_pre), kernel_one).astype(jnp.bfloat16)
    piece = lax.all_gather(grad_embedded, "code", axis=0, tiled=True)
    code_terms = lax.dot_general(
        weights.reshape(-1, code_slice),
        piece.reshape(-1, piece.shape[2]),
        (((0,), (0,)), ((), ())),
        preferred_element_type=jnp.float32,
    )
    grad_codebook = lax.psum(code_terms.astype(jnp.bfloat16), ("space", "clip")).astype(jnp.float32)
    term_two = kernel_grad(hidden_pad, upstream)
    term_one = kernel_grad(embed_pad, grad_pre)
    grad_one, grad_two = (
        lax.psum_scatter(term_one, ("space", "code", "clip"), scatter_dimension=3, tiled=True),
        lax.psum_scatter(term_two, ("space", "code", "clip"), scatter_dimension=3, tiled=True),
    )
    return (decoded[None], grad_one, grad_two, grad_codebook)


def solution(mesh):
    in_specs = (
        P("clip", "space", None, "code"),
        P("code", None),
        P(),
        P(),
        P("clip", ("space", "code"), None, None),
    )
    out_specs = (
        P("clip", ("space", "code"), None, None),
        P(None, None, None, ("space", "code", "clip")),
        P(None, None, None, ("space", "code", "clip")),
        P("code", None),
    )
    return jax.shard_map(
        on_device, mesh=mesh, in_specs=in_specs, out_specs=out_specs, check_vma=False
    )
```

profile of v0, /device:TPU:1, one launch (start us, length us, event | category | flops | bytes accessed | tf_op | source)
XLA Modules:
  0.0 509.3 jit_solution(13997313864569233537)
XLA Ops:
  8.4 5.7 %fusion = f32[64,32,256]{2,1,0:T(8,128)S(1)} fusion(bf16[1,64,32,2048]{3,2,1,0:T(8,128)(2,1)} %param.5, bf16[2048,256]{1,0:T(8,128)(2,1)S(1)} %copy-done), kind=kOutput, calls=%fused_computation.1 | convolution fusion | flops 2147483648 | bytes 11534336 | tf_op jit(solution)/shard_map/dot_general | solution.py:81
  14.1 44.1 %all-reduce.14 = bf16[64,32,256]{2,1,0:T(8,128)(2,1)} all-reduce(f32[64,32,256]{2,1,0:T(8,128)S(1)} %fusion), channel_id=1, replica_groups=mesh['space'=16,'code'=4,'clip'=2] {'code'}, use_global_device_ids=true, to_apply=%region_0.0 | all-reduce | flops 524288 | bytes 3145728 | tf_op jit(solution)/shard_map/psum | solution.py:85
  59.4 1.9 collective-permute-start
  61.3 5.2 %collective-permute-start.1 = (bf16[1,32,256]{2,1,0:T(8,128)(2,1)S(1)}, bf16[1,32,256]{2,1,0:T(8,128)(2,1)S(1)}, u32[]{:S(2)}, u32[]{:S(2)}) collective-permute-start(bf16[1,32,256]{2,1,0:T(8,128)(2,1)S(1)} %get-tuple-element.55), channel_id=1, source_target_pairs={{2,0},{4,2},{6,4},{8,6},{10,8},{12,10},{14,12},{16,14},{18,16},{20... | collective-permute-start | bytes 49160 | tf_op jit(solution)/shard_map/ppermute | solution.py:15
  66.5 1.9 collective-permute-start.4
  68.5 4.9 collective-permute-start.5
  76.5 1.5 convolution_bitcast_fusion.4
  88.3 1.9 collective-permute-start.2
  90.2 4.9 collective-permute-start.3
  95.0 1.9 collective-permute-start.6
  97.0 5.0 collective-permute-start.7
  103.2 2.7 pad_maximum_fusion.1
  105.8 7.3 %copy.12 = f32[3,3,256,512]{2,1,0,3:T(4,128)} copy(f32[3,3,256,512]{3,2,1,0:T(8,128)} %pad_maximum_fusion.1) | data formatting | bytes 9437184 | tf_op jit(solution)/shard_map/stack | solution.py:72
  113.4 2.0 fusion.114
  127.8 3.4 maximum_bitcast_fusion
  131.2 27.6 %all-gather.2.cloned.1.call-done = bf16[64,32,256]{2,1,0:T(8,128)(2,1)} async-done(((bf16[16,32,256]{2,1,0:T(8,128)(2,1)}), bf16[64,32,256]{2,1,0:T(8,128)(2,1)}) %all-gather.2.cloned.1.call-update) | async-done | bytes 1048592 | tf_op jit(solution)/shard_map/all_gather | solution.py:97
  158.8 7.0 %fusion.2 = bf16[2048,256]{0,1:T(8,128)(2,1)} fusion(bf16[2048,256]{1,0:T(8,128)(2,1)} %bitcast.297, bf16[2048,2048]{1,0:T(8,128)(2,1)} %bitcast.275), kind=kOutput, calls=%fused_computation.8 | convolution fusion | flops 2148007936 | bytes 10485760 | tf_op jit(solution)/shard_map/dot_general | solution.py:98
  166.1 2.3 maximum_bitcast_fusion.2
  169.9 4.7 pad_maximum_fusion
  174.6 13.8 %copy.13 = f32[3,3,512,512]{2,1,0,3:T(4,128)} copy(f32[3,3,512,512]{3,2,1,0:T(8,128)} %pad_maximum_fusion) | data formatting | bytes 18874368 | tf_op jit(solution)/shard_map/stack | solution.py:72
  188.5 1.7 fusion.32
  190.2 1.5 fusion.14
  191.7 1.5 convolution_add_fusion.13
  193.2 1.5 convolution_add_fusion.12
  194.7 1.6 convolution_add_fusion.11
  196.3 1.5 convolution_add_fusion.10
  197.8 1.5 convolution_add_fusion.9
  199.3 1.5 convolution_add_fusion.8
  200.8 2.4 fusion.7
  203.2 70.1 %all-reduce.11.cloned.1.call-done = bf16[2048,256]{0,1:T(8,128)(2,1)} async-done(((bf16[2048,256]{0,1:T(8,128)(2,1)}), bf16[2048,256]{0,1:T(8,128)(2,1)}) %all-reduce.11.cloned.1.call-update) | async-done | bytes 1048592 | tf_op jit(solution)/shard_map/psum | solution.py:104
  273.2 2.6 copy.16
  275.8 223.9 %all-reduce.13.cloned.1.call-done = (f32[3,3,256,512]{2,1,0,3:T(4,128)}, f32[3,3,512,512]{2,1,0,3:T(4,128)}) async-done(((f32[3,3,256,512]{2,1,0,3:T(4,128)}, f32[3,3,512,512]{2,1,0,3:T(4,128)}), (f32[3,3,256,512]{2,1,0,3:T(4,128)}, f32[3,3,512,512]{2,1,0,3:T(4,128)})) %all-reduce.13.cloned.1.call-update) | async-done | bytes 14155792
  (136 shorter events, 33.8 us)
Async XLA Ops:
  7.2 151.6 %all-gather.2.cloned.1.call-start = ((), (), s32[]{:S(2)}) async-start(), calls=%async_computation | async-start | bytes 1310720 | tf_op jit(solution)/shard_map/all_gather | solution.py:97
  14.1 52.4 %copy-start.2 = (bf16[1,16,32,512]{3,2,1,0:T(8,128)(2,1)S(1)}, bf16[1,16,32,512]{3,2,1,0:T(8,128)(2,1)}, u32[]{:S(2)}) copy-start(bf16[1,16,32,512]{3,2,1,0:T(8,128)(2,1)} %param.9) | copy-start | bytes 1572868
  58.3 15.5 %copy-start.5 = (bf16[3,3,256,512]{3,2,1,0:T(8,128)(2,1)S(1)}, bf16[3,3,256,512]{3,2,1,0:T(8,128)(2,1)}, u32[]{:S(2)}) copy-start(bf16[3,3,256,512]{3,2,1,0:T(8,128)(2,1)} %param.7) | copy-start | bytes 7077892
  59.4 13.9 %collective-permute-start = (bf16[1,32,256]{2,1,0:T(8,128)(2,1)S(1)}, bf16[1,32,256]{2,1,0:T(8,128)(2,1)S(1)}, u32[]{:S(2)}, u32[]{:S(2)}) collective-permute-start(bf16[1,32,256]{2,1,0:T(8,128)(2,1)S(1)} %get-tuple-element.54), channel_id=1, source_target_pairs={{0,2},{2,4},{4,6},{6,8},{8,10},{10,12},{12,14},{14,16},{16,18},{18... | collective-permute-start | bytes 49160 | tf_op jit(solution)/shard_map/ppermute | solution.py:12
  61.3 12.0 %collective-permute-start.1 = (bf16[1,32,256]{2,1,0:T(8,128)(2,1)S(1)}, bf16[1,32,256]{2,1,0:T(8,128)(2,1)S(1)}, u32[]{:S(2)}, u32[]{:S(2)}) collective-permute-start(bf16[1,32,256]{2,1,0:T(8,128)(2,1)S(1)} %get-tuple-element.55), channel_id=1, source_target_pairs={{2,0},{4,2},{6,4},{8,6},{10,8},{12,10},{14,12},{16,14},{18,16},{20... | collective-permute-start | bytes 49160 | tf_op jit(solution)/shard_map/ppermute | solution.py:15
  66.5 11.5 %collective-permute-start.4 = (bf16[1,32,512]{2,1,0:T(8,128)(2,1)S(1)}, bf16[1,32,512]{2,1,0:T(8,128)(2,1)S(1)}, u32[]{:S(2)}, u32[]{:S(2)}) collective-permute-start(bf16[1,32,512]{2,1,0:T(8,128)(2,1)S(1)} %get-tuple-element.40), channel_id=1, source_target_pairs={{0,2},{2,4},{4,6},{6,8},{8,10},{10,12},{12,14},{14,16},{16,18},{18... | collective-permute-start | bytes 98312 | tf_op jit(solution)/shard_map/ppermute | solution.py:12
  68.5 9.6 %collective-permute-start.5 = (bf16[1,32,512]{2,1,0:T(8,128)(2,1)S(1)}, bf16[1,32,512]{2,1,0:T(8,128)(2,1)S(1)}, u32[]{:S(2)}, u32[]{:S(2)}) collective-permute-start(bf16[1,32,512]{2,1,0:T(8,128)(2,1)S(1)} %get-tuple-element.41), channel_id=1, source_target_pairs={{2,0},{4,2},{6,4},{8,6},{10,8},{12,10},{14,12},{16,14},{18,16},{20... | collective-permute-start | bytes 98312 | tf_op jit(solution)/shard_map/ppermute | solution.py:15
  76.5 7.6 %copy-start.19 = (f32[512,512]{1,0:T(8,128)}, f32[512,512]{1,0:T(8,128)S(1)}, u32[]{:S(2)}) copy-start(f32[512,512]{1,0:T(8,128)S(1)} %fusion.6) | copy-start | bytes 3145732
  76.5 2.9 slice-start
  78.0 1.7 slice-start.1
  84.6 3.0 copy-start.6
  84.6 17.8 %copy-start.8 = (bf16[16,32,512]{2,1,0:T(8,128)(2,1)}, bf16[16,32,512]{2,1,0:T(8,128)(2,1)S(1)}, u32[]{:S(2)}) copy-start(bf16[16,32,512]{2,1,0:T(8,128)(2,1)S(1)} %get-tuple-element.14) | copy-start | bytes 1572868
  88.3 24.8 %collective-permute-start.2 = (bf16[1,32,512]{2,1,0:T(8,128)(2,1)}, bf16[1,32,512]{2,1,0:T(8,128)(2,1)S(1)}, u32[]{:S(2)}, u32[]{:S(2)}) collective-permute-start(bf16[1,32,512]{2,1,0:T(8,128)(2,1)} %get-tuple-element.44), channel_id=1, source_target_pairs={{0,2},{2,4},{4,6},{6,8},{8,10},{10,12},{12,14},{14,16},{16,18},{18... | collective-permute-start | bytes 98312 | tf_op jit(solution)/shard_map/ppermute | solution.py:12
  90.2 22.9 %collective-permute-start.3 = (bf16[1,32,512]{2,1,0:T(8,128)(2,1)}, bf16[1,32,512]{2,1,0:T(8,128)(2,1)S(1)}, u32[]{:S(2)}, u32[]{:S(2)}) collective-permute-start(bf16[1,32,512]{2,1,0:T(8,128)(2,1)} %get-tuple-element.45), channel_id=1, source_target_pairs={{2,0},{4,2},{6,4},{8,6},{10,8},{12,10},{14,12},{16,14},{18,16},{20... | collective-permute-start | bytes 98312 | tf_op jit(solution)/shard_map/ppermute | solution.py:15
  95.0 20.3 %collective-permute-start.6 = (bf16[1,32,512]{2,1,0:T(8,128)(2,1)}, bf16[1,32,512]{2,1,0:T(8,128)(2,1)S(1)}, u32[]{:S(2)}, u32[]{:S(2)}) collective-permute-start(bf16[1,32,512]{2,1,0:T(8,128)(2,1)} %get-tuple-element.36), channel_id=1, source_target_pairs={{0,2},{2,4},{4,6},{6,8},{8,10},{10,12},{12,14},{14,16},{16,18},{18... | collective-permute-start | bytes 98312 | tf_op jit(solution)/shard_map/ppermute | solution.py:12
  97.0 18.4 %collective-permute-start.7 = (bf16[1,32,512]{2,1,0:T(8,128)(2,1)}, bf16[1,32,512]{2,1,0:T(8,128)(2,1)S(1)}, u32[]{:S(2)}, u32[]{:S(2)}) collective-permute-start(bf16[1,32,512]{2,1,0:T(8,128)(2,1)} %get-tuple-element.37), channel_id=1, source_target_pairs={{2,0},{4,2},{6,4},{8,6},{10,8},{12,10},{14,12},{16,14},{18,16},{20... | collective-permute-start | bytes 98312 | tf_op jit(solution)/shard_map/ppermute | solution.py:15
  105.8 7.3 %copy-start.7 = (bf16[16,32,512]{2,1,0:T(8,128)(2,1)S(1)}, bf16[16,32,512]{2,1,0:T(8,128)(2,1)}, u32[]{:S(2)}) copy-start(bf16[16,32,512]{2,1,0:T(8,128)(2,1)} %copy-done.6) | copy-start | bytes 1572868
  113.4 2.0 copy-start.9
  120.8 152.5 %all-reduce.11.cloned.1.call-start = ((), (), s32[]{:S(2)}) async-start(), calls=%async_computation.1 | async-start | bytes 2097152 | tf_op jit(solution)/shard_map/psum | solution.py:104
  120.9 2.4 copy-start.17
  120.9 1.9 copy-start.11
  121.4 1.9 copy-start.10
  122.9 1.9 copy-start.12
  123.3 1.9 copy-start.13
  125.7 2.0 copy-start.24
  165.8 333.9 %all-reduce.13.cloned.1.call-start = ((), (), s32[]{:S(2)}) async-start(), calls=%async_computation.2 | async-start | bytes 37748736
  166.1 2.8 copy-start.3
  166.1 3.8 copy-start.4
  188.5 1.7 copy-start.15
  188.5 3.2 copy-start.18
  194.7 1.6 copy-start.21
  200.8 302.0 %copy-start.1 = (bf16[2048,256]{1,0:T(8,128)(2,1)S(1)}, bf16[2048,256]{1,0:T(8,128)(2,1)}, u32[]{:S(2)}) copy-start(bf16[2048,256]{1,0:T(8,128)(2,1)} %param.6) | copy-start | bytes 3145732
  (6 other events, 7.7 us)
Sparse Core Ops, SparseCore 0:
  120.9 37.8 all-gather.1
  166.0 107.2 all-reduce.10
  278.8 220.8 all-reduce.12
where the time goes:
time: 511 us; the launch traced here: 509 us
  waiting for transfers between devices  322 us (63%)
  matrix products  49.1 us (10%)
  blocking collectives  44.1 us (9%)
  local copies, waits for them, and re-layouts  36.6 us (7%)
  starting transfers between devices  27.9 us (5%)
  other arithmetic  15.2 us (3%)
  between operations  14.6 us (3%)
    unnamed x4, waiting for transfers between devices  224 us
    psum x1, waiting for transfers between devices, on_device(): lax.psum(code_terms.astype(jnp.bfloat16), ('space', 'clip'))  70.1 us
    psum x1, blocking collectives, on_device(): summed = lax.psum(partial_value, 'code')  44.1 us
    all_gather x1, waiting for transfers between devices, on_device(): piece = lax.all_gather(grad_embedded, 'code', axis=0, tiled=True)  27.6 us
    another operation x2, local copies, waits for them, and re-layouts, kernel_grad(): return jnp.stack(result)  21.1 us
    ppermute x4, starting transfers between devices, with_halo(): lax.ppermute(lax.slice_in_dim(block, 0, width, axis=dim), axis, backward)  19.9 us
    dot_general x18, matrix products, taps_forward(): jnp.dot(window, kernel[first, second], preferred_element_type=jnp.float32)  17.2 us
    another operation x6, other arithmetic, kernel_grad(): return jnp.stack(result)  13.6 us
  transfers between devices with their start and end apart: 11, of which 3 were waited for; matrix products, arithmetic and copies ran while one was open for 13% of the time, Pallas kernels for 0%

commit v1 on v0

--- a/solution.py
+++ b/solution.py
@@ -82,7 +82,9 @@
         weights.reshape(-1, code_slice), codebook, preferred_element_type=jnp.float32
     )
     partial_value = partial_value.reshape(weights.shape[0], breadth, -1)
-    summed = lax.psum(partial_value, "code")
+    summed = partial_value
+    for hop in (1, 2):
+        summed = summed + lax.ppermute(summed, "code", [(dev, dev ^ hop) for dev in range(4)])
     owned = lax.dynamic_slice_in_dim(summed, lax.axis_index("code") * own_rows, own_rows, 0)
     embedded = owned.astype(jnp.bfloat16)
     embed_pad = extend(embedded)

time: 511 us -> 553 us (1.082)
  waiting for transfers between devices: 322 us -> 396 us
  blocking collectives: 44.1 us -> 0 us
  starting transfers between devices: 27.9 us -> 35.5 us
    psum x1 -> x0, blocking collectives: 44.1 us -> none  [on_device(): summed = lax.psum(partial_value, 'code')]
    ppermute x0 -> x2, waiting for transfers between devices: none -> 41.2 us  [on_device(): lax.ppermute(summed, 'code', [(dev, dev ^ hop) for dev in range(4)])]
    ppermute x4, waiting for transfers between devices: 0.01 us -> 38.3 us  [with_halo(): lax.ppermute(lax.slice_in_dim(block, block.shape[dim] - width, None, axis...]
    all_gather x1, waiting for transfers between devices: 27.6 us -> 21 us  [on_device(): piece = lax.all_gather(grad_embedded, 'code', axis=0, tiled=True)]
    ppermute x0 -> x2, starting transfers between devices: none -> 5.67 us  [on_device(): lax.ppermute(summed, 'code', [(dev, dev ^ hop) for dev in range(4)])]
    unnamed x59 -> x49, local copies, waits for them, and re-layouts: 9.85 us -> 13.5 us
  transfers between devices with their start and end apart: 11 -> 13, of which waited for: 3 -> 7; matrix products, arithmetic and copies ran while one was open for 13% -> 12% of each run, Pallas kernels for 0% -> 0%
where the time goes in v1:
time: 553 us; the launch traced here: 552 us
  waiting for transfers between devices  396 us (72%)
  matrix products  50.5 us (9%)
  local copies, waits for them, and re-layouts  37.5 us (7%)
  starting transfers between devices  35.5 us (6%)
  other arithmetic  17.9 us (3%)
  between operations  14.5 us (3%)
    unnamed x4, waiting for transfers between devices  224 us
    psum x1, waiting for transfers between devices, on_device(): lax.psum(code_terms.astype(jnp.bfloat16), ('space', 'clip'))  70.1 us
    ppermute x2, waiting for transfers between devices, on_device(): lax.ppermute(summed, 'code', [(dev, dev ^ hop) for dev in range(4)])  41.2 us
    ppermute x4, waiting for transfers between devices, with_halo(): lax.ppermute(lax.slice_in_dim(block, block.shape[dim] - width, None, axis...  38.3 us
    another operation x2, local copies, waits for them, and re-layouts, kernel_grad(): return jnp.stack(result)  21.1 us
    ppermute x4, starting transfers between devices, with_halo(): lax.ppermute(lax.slice_in_dim(block, 0, width, axis=dim), axis, backward)  21.1 us
    all_gather x1, waiting for transfers between devices, on_device(): piece = lax.all_gather(grad_embedded, 'code', axis=0, tiled=True)  21 us
    dot_general x18, matrix products, taps_forward(): jnp.dot(window, kernel[first, second], preferred_element_type=jnp.float32)  17.2 us
  transfers between devices with their start and end apart: 13, of which 7 were waited for; matrix products, arithmetic and copies ran while one was open for 12% of the time, Pallas kernels for 0%

profile of v1, /device:TPU:1, one launch (start us, length us, event | category | flops | bytes accessed | tf_op | source)
XLA Modules:
  0.0 551.9 jit_solution(4143290019337486907)
XLA Ops:
  8.4 7.1 %fusion = f32[64,32,256]{2,1,0:T(8,128)} fusion(bf16[1,64,32,2048]{3,2,1,0:T(8,128)(2,1)} %param.5, bf16[2048,256]{1,0:T(8,128)(2,1)S(1)} %copy-done), kind=kOutput, calls=%fused_computation.1 | convolution fusion | flops 2147483648 | bytes 11534336 | tf_op jit(solution)/shard_map/dot_general | solution.py:81
  15.5 2.5 collective-permute-start
  17.9 1.9 collective-permute-start.6
  19.8 5.0 collective-permute-start.7
  24.9 38.3 %collective-permute-done.6 = bf16[1,32,512]{2,1,0:T(8,128)(2,1)S(1)} collective-permute-done((bf16[1,32,512]{2,1,0:T(8,128)(2,1)S(1)}, bf16[1,32,512]{2,1,0:T(8,128)(2,1)S(1)}, u32[]{:S(2)}, u32[]{:S(2)}) %collective-permute-start.6) | collective-permute-done | bytes 32800 | tf_op jit(solution)/shard_map/ppermute | solution.py:12
  65.1 1.8 copy-done.3
  67.4 2.6 add.134
  70.0 3.2 collective-permute-start.1
  76.6 41.2 %collective-permute-done.1 = f32[64,32,256]{2,1,0:T(8,128)S(1)} collective-permute-done((f32[64,32,256]{2,1,0:T(8,128)S(1)}, f32[64,32,256]{2,1,0:T(8,128)S(1)}, u32[]{:S(2)}, u32[]{:S(2)}) %collective-permute-start.1) | collective-permute-done | bytes 2097184 | tf_op jit(solution)/shard_map/ppermute | solution.py:87
  117.9 2.6 collective-permute-start.2
  120.6 6.2 %collective-permute-start.3 = (bf16[1,32,256]{2,1,0:T(8,128)(2,1)S(1)}, bf16[1,32,256]{2,1,0:T(8,128)(2,1)S(1)}, u32[]{:S(2)}, u32[]{:S(2)}) collective-permute-start(bf16[1,32,256]{2,1,0:T(8,128)(2,1)S(1)} %get-tuple-element.55), channel_id=1, source_target_pairs={{2,0},{4,2},{6,4},{8,6},{10,8},{12,10},{14,12},{16,14},{18,16},{20... | collective-permute-start | bytes 49160 | tf_op jit(solution)/shard_map/ppermute | solution.py:15
  132.1 1.5 convolution_bitcast_fusion.4
  136.5 1.9 collective-permute-start.4
  138.4 4.9 collective-permute-start.5
  143.3 1.9 collective-permute-start.8
  145.2 5.0 collective-permute-start.9
  151.3 2.7 pad_maximum_fusion.1
  154.0 7.3 %copy.12 = f32[3,3,256,512]{2,1,0,3:T(4,128)} copy(f32[3,3,256,512]{3,2,1,0:T(8,128)} %pad_maximum_fusion.1) | data formatting | bytes 9437184 | tf_op jit(solution)/shard_map/stack | solution.py:72
  161.5 1.6 fusion.115
  177.0 3.4 maximum_bitcast_fusion
  180.4 21.0 %all-gather.2.cloned.1.call-done = bf16[64,32,256]{2,1,0:T(8,128)(2,1)} async-done(((bf16[16,32,256]{2,1,0:T(8,128)(2,1)}), bf16[64,32,256]{2,1,0:T(8,128)(2,1)}) %all-gather.2.cloned.1.call-update) | async-done | bytes 1048592 | tf_op jit(solution)/shard_map/all_gather | solution.py:99
  201.4 7.1 %fusion.2 = bf16[2048,256]{0,1:T(8,128)(2,1)} fusion(bf16[2048,256]{1,0:T(8,128)(2,1)} %bitcast.295, bf16[2048,2048]{1,0:T(8,128)(2,1)} %bitcast.275), kind=kOutput, calls=%fused_computation.8 | convolution fusion | flops 2148007936 | bytes 10485760 | tf_op jit(solution)/shard_map/dot_general | solution.py:100
  208.7 2.3 maximum_bitcast_fusion.2
  212.5 4.7 pad_maximum_fusion
  217.2 13.8 %copy.13 = f32[3,3,512,512]{2,1,0,3:T(4,128)} copy(f32[3,3,512,512]{3,2,1,0:T(8,128)} %pad_maximum_fusion) | data formatting | bytes 18874368 | tf_op jit(solution)/shard_map/stack | solution.py:72
  231.1 1.7 fusion.33
  237.3 1.6 convolution_add_fusion.11
  238.9 1.5 convolution_add_fusion.10
  243.4 2.4 fusion.7
  245.8 70.1 %all-reduce.10.cloned.1.call-done = bf16[2048,256]{0,1:T(8,128)(2,1)} async-done(((bf16[2048,256]{0,1:T(8,128)(2,1)}), bf16[2048,256]{0,1:T(8,128)(2,1)}) %all-reduce.10.cloned.1.call-update) | async-done | bytes 1048592 | tf_op jit(solution)/shard_map/psum | solution.py:106
  315.9 2.6 copy.16
  318.5 223.9 %all-reduce.12.cloned.1.call-done = (f32[3,3,256,512]{2,1,0,3:T(4,128)}, f32[3,3,512,512]{2,1,0,3:T(4,128)}) async-done(((f32[3,3,256,512]{2,1,0,3:T(4,128)}, f32[3,3,512,512]{2,1,0,3:T(4,128)}), (f32[3,3,256,512]{2,1,0,3:T(4,128)}, f32[3,3,512,512]{2,1,0,3:T(4,128)})) %all-reduce.12.cloned.1.call-update) | async-done | bytes 14155792
  (129 shorter events, 42.1 us)
Async XLA Ops:
  7.2 1.2 copy-start
  7.2 10.7 %copy-start.2 = (bf16[1,16,32,512]{3,2,1,0:T(8,128)(2,1)S(1)}, bf16[1,16,32,512]{3,2,1,0:T(8,128)(2,1)}, u32[]{:S(2)}) copy-start(bf16[1,16,32,512]{3,2,1,0:T(8,128)(2,1)} %param.9) | copy-start | bytes 1572868
  7.2 194.2 %all-gather.2.cloned.1.call-start = ((), (), s32[]{:S(2)}) async-start(), calls=%async_computation | async-start | bytes 1310720 | tf_op jit(solution)/shard_map/all_gather | solution.py:99
  15.5 52.0 %collective-permute-start = (f32[64,32,256]{2,1,0:T(8,128)}, f32[64,32,256]{2,1,0:T(8,128)}, u32[]{:S(2)}, u32[]{:S(2)}) collective-permute-start(f32[64,32,256]{2,1,0:T(8,128)} %fusion), channel_id=1, source_target_pairs={{0,2},{2,0},{4,6},{6,4},{1,3},{3,1},{5,7},{7,5},{8,10},{10,8},{12,... | collective-permute-start | bytes 6291464 | tf_op jit(solution)/shard_map/ppermute | solution.py:87
  17.9 45.2 %collective-permute-start.6 = (bf16[1,32,512]{2,1,0:T(8,128)(2,1)S(1)}, bf16[1,32,512]{2,1,0:T(8,128)(2,1)S(1)}, u32[]{:S(2)}, u32[]{:S(2)}) collective-permute-start(bf16[1,32,512]{2,1,0:T(8,128)(2,1)S(1)} %get-tuple-element.40), channel_id=1, source_target_pairs={{0,2},{2,4},{4,6},{6,8},{8,10},{10,12},{12,14},{14,16},{16,18},{18... | collective-permute-start | bytes 98312 | tf_op jit(solution)/shard_map/ppermute | solution.py:12
  19.8 44.4 %collective-permute-start.7 = (bf16[1,32,512]{2,1,0:T(8,128)(2,1)S(1)}, bf16[1,32,512]{2,1,0:T(8,128)(2,1)S(1)}, u32[]{:S(2)}, u32[]{:S(2)}) collective-permute-start(bf16[1,32,512]{2,1,0:T(8,128)(2,1)S(1)} %get-tuple-element.41), channel_id=1, source_target_pairs={{2,0},{4,2},{6,4},{8,6},{10,8},{12,10},{14,12},{16,14},{18,16},{20... | collective-permute-start | bytes 98312 | tf_op jit(solution)/shard_map/ppermute | solution.py:15
  64.6 2.3 copy-start.3
  70.0 47.8 %collective-permute-start.1 = (f32[64,32,256]{2,1,0:T(8,128)S(1)}, f32[64,32,256]{2,1,0:T(8,128)S(1)}, u32[]{:S(2)}, u32[]{:S(2)}) collective-permute-start(f32[64,32,256]{2,1,0:T(8,128)S(1)} %add.134), channel_id=1, source_target_pairs={{0,4},{2,6},{4,0},{6,2},{1,5},{3,7},{5,1},{7,3},{8,12},{10,14},{12... | collective-permute-start | bytes 6291464 | tf_op jit(solution)/shard_map/ppermute | solution.py:87
  117.9 9.4 %collective-permute-start.2 = (bf16[1,32,256]{2,1,0:T(8,128)(2,1)S(1)}, bf16[1,32,256]{2,1,0:T(8,128)(2,1)S(1)}, u32[]{:S(2)}, u32[]{:S(2)}) collective-permute-start(bf16[1,32,256]{2,1,0:T(8,128)(2,1)S(1)} %get-tuple-element.54), channel_id=1, source_target_pairs={{0,2},{2,4},{4,6},{6,8},{8,10},{10,12},{12,14},{14,16},{16,18},{18... | collective-permute-start | bytes 49160 | tf_op jit(solution)/shard_map/ppermute | solution.py:12
  120.6 7.0 %collective-permute-start.3 = (bf16[1,32,256]{2,1,0:T(8,128)(2,1)S(1)}, bf16[1,32,256]{2,1,0:T(8,128)(2,1)S(1)}, u32[]{:S(2)}, u32[]{:S(2)}) collective-permute-start(bf16[1,32,256]{2,1,0:T(8,128)(2,1)S(1)} %get-tuple-element.55), channel_id=1, source_target_pairs={{2,0},{4,2},{6,4},{8,6},{10,8},{12,10},{14,12},{16,14},{18,16},{20... | collective-permute-start | bytes 49160 | tf_op jit(solution)/shard_map/ppermute | solution.py:15
  127.3 6.3 %copy-start.19 = (f32[512,512]{1,0:T(8,128)}, f32[512,512]{1,0:T(8,128)S(1)}, u32[]{:S(2)}) copy-start(f32[512,512]{1,0:T(8,128)S(1)} %fusion.4) | copy-start | bytes 3145732
  127.3 2.0 copy-start.6
  132.1 1.5 copy-start.16
  136.5 24.8 %collective-permute-start.4 = (bf16[1,32,512]{2,1,0:T(8,128)(2,1)S(1)}, bf16[1,32,512]{2,1,0:T(8,128)(2,1)S(1)}, u32[]{:S(2)}, u32[]{:S(2)}) collective-permute-start(bf16[1,32,512]{2,1,0:T(8,128)(2,1)S(1)} %get-tuple-element.44), channel_id=1, source_target_pairs={{0,2},{2,4},{4,6},{6,8},{8,10},{10,12},{12,14},{14,16},{16,18},{18... | collective-permute-start | bytes 98312 | tf_op jit(solution)/shard_map/ppermute | solution.py:12
  138.4 22.9 %collective-permute-start.5 = (bf16[1,32,512]{2,1,0:T(8,128)(2,1)S(1)}, bf16[1,32,512]{2,1,0:T(8,128)(2,1)S(1)}, u32[]{:S(2)}, u32[]{:S(2)}) collective-permute-start(bf16[1,32,512]{2,1,0:T(8,128)(2,1)S(1)} %get-tuple-element.45), channel_id=1, source_target_pairs={{2,0},{4,2},{6,4},{8,6},{10,8},{12,10},{14,12},{16,14},{18,16},{20... | collective-permute-start | bytes 98312 | tf_op jit(solution)/shard_map/ppermute | solution.py:15
  143.3 19.9 %collective-permute-start.8 = (bf16[1,32,512]{2,1,0:T(8,128)(2,1)S(1)}, bf16[1,32,512]{2,1,0:T(8,128)(2,1)S(1)}, u32[]{:S(2)}, u32[]{:S(2)}) collective-permute-start(bf16[1,32,512]{2,1,0:T(8,128)(2,1)S(1)} %get-tuple-element.36), channel_id=1, source_target_pairs={{0,2},{2,4},{4,6},{6,8},{8,10},{10,12},{12,14},{14,16},{16,18},{18... | collective-permute-start | bytes 98312 | tf_op jit(solution)/shard_map/ppermute | solution.py:12
  145.2 18.0 %collective-permute-start.9 = (bf16[1,32,512]{2,1,0:T(8,128)(2,1)S(1)}, bf16[1,32,512]{2,1,0:T(8,128)(2,1)S(1)}, u32[]{:S(2)}, u32[]{:S(2)}) collective-permute-start(bf16[1,32,512]{2,1,0:T(8,128)(2,1)S(1)} %get-tuple-element.37), channel_id=1, source_target_pairs={{2,0},{4,2},{6,4},{8,6},{10,8},{12,10},{14,12},{16,14},{18,16},{20... | collective-permute-start | bytes 98312 | tf_op jit(solution)/shard_map/ppermute | solution.py:15
  163.4 1.7 copy-start.7
  165.5 1.2 copy-start.17
  165.5 1.5 copy-start.20
  169.7 146.2 %all-reduce.10.cloned.1.call-start = ((), (), s32[]{:S(2)}) async-start(), calls=%async_computation.1 | async-start | bytes 2097152 | tf_op jit(solution)/shard_map/psum | solution.py:106
  169.9 2.3 copy-start.8
  172.1 1.9 copy-start.9
  172.6 1.9 copy-start.10
  175.0 2.0 copy-start.21
  208.5 333.9 %all-reduce.12.cloned.1.call-start = ((), (), s32[]{:S(2)}) async-start(), calls=%async_computation.2 | async-start | bytes 37748736
  208.7 2.8 copy-start.4
  208.7 3.8 copy-start.5
  231.1 1.7 copy-start.12
  231.1 3.2 copy-start.15
  237.3 1.6 copy-start.18
  243.4 302.0 %copy-start.1 = (bf16[2048,256]{1,0:T(8,128)(2,1)S(1)}, bf16[2048,256]{1,0:T(8,128)(2,1)}, u32[]{:S(2)}) copy-start(bf16[2048,256]{1,0:T(8,128)(2,1)} %param.6) | copy-start | bytes 3145732
  (3 other events, 2.9 us)
Sparse Core Ops, SparseCore 0:
  169.8 31.4 all-gather.1
  208.6 107.2 all-reduce.9
  321.5 220.8 all-reduce.11
